TPU v7x, 1024 devices: a whole 8x8x8 slice. The times are simulated.
1024 devices in a mesh: section: 8 (over x), ctx: 8 (over z), exp: 16 (over y, core).
Axes of the slice: x: 8, y: 8, z: 8, core: 2. Of those that a mesh axis runs over, the one named last changes fastest.
Arguments:
- queries: bfloat16 [8, 2048, 8192], P('section', 'ctx', 'exp'), may hold values from -0.8984375 to 0.8984375
- keys_in: bfloat16 [8, 2048, 8192], P('section', 'ctx', 'exp'), may hold values from -0.8984375 to 0.8984375
- values: bfloat16 [8, 2048, 8192], P('section', 'ctx', 'exp'), may hold values from -6 to 6
- decay_rate: float32 [8, 64, 2048], P('section', 'exp', 'ctx'), may hold values from 0 to 1
- out_weight: bfloat16 [8, 8192, 6144], P('section', 'exp'), may hold values from -0.0625 to 0.0625
- residual: bfloat16 [8, 2048, 6144], P('section', ('ctx', 'exp')), may hold values from -6 to 6
- norm_gain: float32 [8, 6144], P('section'), may hold values from 0.5 to 1.5
- router: bfloat16 [8, 6144, 16], P('section'), may hold values from -0.078125 to 0.078125
- expert_ids: int32 [8, 2048, 2], P('section', ('ctx', 'exp')), may hold values from 0 to 15, all different within a row; in each aligned block of 16 rows (0 to 15, 16 to 31, ..., all dimensions but the last counted through in order) at most 4 rows name the same one
Outputs:
- expert_rows: bfloat16 [8, 8, 16, 16, 4, 6144], P('section', 'ctx', 'exp')
- expert_gates: bfloat16 [8, 8, 16, 16, 4], P('section', 'ctx', 'exp')
Inputs may be any that keep to these rules, and one draw needn't show every extreme that they name: `expert_ids`: in each device's 16 rows, every row names two different experts, no expert is named more than 4 times, and in some devices' rows an expert is named exactly 4 times.
All inputs are finite; a program needn't handle non-finite values.
Results may differ from a plain program's by a relative error of at most 0.02.
Values may be sent and summed in bfloat16 or wider, within the bound.
A program may use at most 64 MiB of HBM per device.

v0:
```python
import math

import jax
import jax.numpy as jnp
from jax import lax
from jax.sharding import PartitionSpec as P

HEAD_DIM = 128
HEAD_DEV = 4
EXPERTS = 16
CAP = 4


epsilon = 1e-05


def side_by_side(arrays, axis, dim, along):
    columns = [a.reshape(*a.shape[:along], -1) for a in arrays]
    both = jnp.concatenate(columns, axis=along)
    whole, at, finished = (lax.all_gather(both, axis, axis=dim, tiled=True), 0, [])
    for a, column in zip(arrays, columns):
        piece = whole[..., at : at + column.shape[along]]
        finished.append(piece.reshape(*piece.shape[:along], *a.shape[along:]))
        at += column.shape[along]
    return tuple(finished)


def from_behind(block, axis, distance):
    devices = range(lax.axis_size(axis))
    route = [((i - distance) % len(devices), i) for i in devices]
    return lax.ppermute(block, axis, route)


def in_one_piece(arrays, axis, split_dim, concat_dim, along):
    widths = [math.prod(a.shape[along:]) for a in arrays]
    both = jnp.concatenate(
        [a.reshape(*a.shape[:along], w) for a, w in zip(arrays, widths)], axis=along
    )
    whole = lax.all_to_all(both, axis, split_axis=split_dim, concat_axis=concat_dim, tiled=True)
    pieces = jnp.split(whole, [sum(widths[:k]) for k in range(1, len(widths))], axis=along)
    return tuple(
        (b.reshape(*whole.shape[:along], *a.shape[along:]) for a, b in zip(arrays, pieces))
    )


def on_device(
    queries, keys_in, values, decay_rate, out_weight, residual, norm_gain, router, expert_ids
):
    seq_len = queries.shape[1]
    query_heads = queries[0].reshape(seq_len, HEAD_DEV, HEAD_DIM)
    key_heads = keys_in[0].reshape(seq_len, HEAD_DEV, HEAD_DIM)
    value_heads = values[0].reshape(seq_len, HEAD_DEV, HEAD_DIM)
    cum_log = jnp.cumsum(-decay_rate[0], axis=-1)
    attention_logits = jnp.einsum(
        "bsx,osx->sbo", query_heads, key_heads, preferred_element_type=jnp.float32
    )
    log_gap = cum_log[:, :, None] - cum_log[:, None, :]
    causal = lax.broadcasted_iota(jnp.int32, (seq_len, seq_len), 0) >= lax.broadcasted_iota(
        jnp.int32, (seq_len, seq_len), 1
    )
    weight_matrix = jnp.where(
        causal, attention_logits * jnp.exp(jnp.minimum(log_gap, 0.0)), 0.0
    ).astype(jnp.bfloat16)
    inner_part = jnp.einsum(
        "nsj,jng->sng", weight_matrix, value_heads, preferred_element_type=jnp.float32
    )
    tail_decay = jnp.exp(cum_log[:, -1:] - cum_log)
    keyed_rows = key_heads.astype(jnp.float32) * jnp.transpose(tail_decay)[:, :, None]
    local_state = jnp.einsum("lha,lhb->hab", keyed_rows, value_heads.astype(jnp.float32))
    total_log = cum_log[:, -1]
    all_logs, all_states = tuple(
        (
            part.astype(jnp.float32)
            for part in side_by_side(
                (total_log[None].astype(jnp.bfloat16), local_state[None].astype(jnp.bfloat16)),
                "ctx",
                0,
                2,
            )
        )
    )
    my_index = lax.axis_index("ctx")
    shard_ids = lax.broadcasted_iota(jnp.int32, (all_logs.shape[0], 1), 0)
    before_sum = jnp.cumsum(all_logs, axis=0) - all_logs
    my_before = jnp.sum(jnp.where(shard_ids == my_index, before_sum, 0.0), axis=0)
    exponent = my_before[None, :] - before_sum - all_logs
    shard_weight = jnp.where(shard_ids < my_index, jnp.exp(jnp.minimum(exponent, 0.0)), 0.0)
    carried = jnp.einsum("ch,chab->hab", shard_weight, all_states)
    outside = jnp.exp(jnp.transpose(cum_log))[:, :, None] * jnp.einsum(
        "lhd,hde->lhe", query_heads.astype(jnp.float32), carried
    )
    attended = (inner_part + outside).astype(jnp.bfloat16).reshape(seq_len, HEAD_DEV * HEAD_DIM)
    projection = out_weight[0]
    my_share = lax.psum_scatter(
        jnp.dot(attended, projection, preferred_element_type=jnp.float32).astype(jnp.bfloat16),
        "exp",
        scatter_dimension=0,
        tiled=True,
    ).astype(jnp.float32)
    hidden = (residual[0].astype(jnp.float32) + my_share).astype(jnp.bfloat16)
    received = from_behind(hidden, "section", 1)
    wide = received.astype(jnp.float32)
    mean_sq = jnp.mean(wide * wide, axis=-1, keepdims=True)
    normed = (wide * lax.rsqrt(mean_sq + epsilon) * norm_gain[0][None, :]).astype(jnp.bfloat16)
    logits = jnp.dot(normed, router[0], preferred_element_type=jnp.float32)
    route_ids = expert_ids[0]
    expert_table = lax.broadcasted_iota(jnp.int32, (1, 1, EXPERTS), 2)
    picked = jnp.sum(
        jnp.where(route_ids[:, :, None] == expert_table, logits[:, None, :], 0.0), axis=-1
    )
    first_gate = jax.nn.sigmoid(picked[:, 0] - picked[:, 1])
    gate_pair = jnp.stack([first_gate, 1.0 - first_gate], axis=-1).astype(jnp.bfloat16)
    flat_ids = route_ids.reshape(-1)
    onehot = (flat_ids[:, None] == expert_table[0]).astype(jnp.int32)
    slot_rank = jnp.sum((jnp.cumsum(onehot, axis=0) - onehot) * onehot, axis=-1)
    exp_count = lax.axis_size("exp")
    per_owner = EXPERTS // exp_count
    target = flat_ids % per_owner * (exp_count * CAP) + flat_ids // per_owner * CAP + slot_rank
    slots_all = EXPERTS * CAP
    placement = (target[None, :] == lax.broadcasted_iota(jnp.int32, (slots_all, 1), 0)).astype(
        jnp.bfloat16
    )
    doubled = jnp.repeat(normed, 2, axis=0)
    send_rows = jnp.dot(placement, doubled, preferred_element_type=jnp.float32).astype(jnp.bfloat16)
    send_rows = send_rows.reshape(per_owner, exp_count, CAP, normed.shape[1])
    send_gates = jnp.dot(
        placement, gate_pair.reshape(-1), preferred_element_type=jnp.float32
    ).astype(jnp.bfloat16)
    send_gates = send_gates.reshape(per_owner, exp_count, CAP)
    owner_rows, owner_gates = in_one_piece((send_rows, send_gates), "exp", 1, 1, 3)
    return (owner_rows[None, None], owner_gates[None, None])


def solution(mesh):
    placed = (
        P("section", "ctx", "exp"),
        P("section", "ctx", "exp"),
        P("section", "ctx", "exp"),
        P("section", "exp", "ctx"),
        P("section", "exp", None),
        P("section", ("ctx", "exp"), None),
        P("section", None),
        P("section", None, None),
        P("section", ("ctx", "exp"), None),
    )
    return jax.shard_map(
        on_device,
        mesh=mesh,
        in_specs=placed,
        out_specs=(
            P("section", "ctx", "exp", None, None, None),
            P("section", "ctx", "exp", None, None),
        ),
        check_vma=False,
    )
```

profile of v0, /device:TPU:1, one launch (start us, length us, event | category | flops | bytes accessed | tf_op | source)
XLA Modules:
  0.0 197.0 jit_solution(9357890817692561291)
XLA Ops:
  7.2 0.7 neg.12
  8.0 1.2 reduce-window.6
  9.2 0.1 slice.29
  9.3 0.1 copy.73
  9.4 0.1 copy.74
  9.7 0.1 copy.89
  9.8 1.1 copy.91
  10.9 1.0 reshape_squeeze.15
  11.9 0.2 convolution_convert_fusion.2
  12.2 0.1 copy.79
  12.3 0.8 pad_maximum_fusion.1
  13.2 1.0 reshape_squeeze.13
  14.3 0.5 convolution_bitcast_fusion.1
  14.8 51.3 %all-gather.2.cloned.1.call-done = bf16[8,4,16385]{2,1,0:T(4,128)(2,1)} async-done(((bf16[1,4,16385]{2,1,0:T(4,128)(2,1)}), bf16[8,4,16385]{2,1,0:T(4,128)(2,1)}) %all-gather.2.cloned.1.call-update) | async-done | bytes 1048656 | tf_op jit(solution)/shard_map/all_gather | solution.py:20
  66.2 0.7 slice.31
  66.9 0.1 copy.90
  67.0 0.2 reduce_window_sum.48
  67.2 1.9 slice.32
  69.1 1.1 reshape.113
  70.2 0.1 select_reduce_fusion.2
  70.3 0.1 exponential_select_fusion
  70.4 0.7 fusion.7
  71.1 0.3 fusion.5
  71.4 6.3 %convolution_convert_fusion = bf16[256,6144]{1,0:T(8,128)(2,1)} fusion(bf16[256,512]{0,1:T(8,128)(2,1)S(1)} %bitcast.67, bf16[1,512,6144]{2,1,0:T(8,128)(2,1)} %param.13), kind=kOutput, calls=%fused_computation | convolution fusion | flops 1612185600 | bytes 9699328 | tf_op jit(solution)/shard_map/dot_general | solution.py:95
  77.7 0.6 copy-done.3
  78.4 0.1 copy.70
  78.4 0.1 reshape_squeeze.12
  78.7 0.2 select_reduce_fusion.1
  78.8 67.8 %reduce-scatter.2.cloned.1.call-done = bf16[16,6144]{1,0:T(8,128)(2,1)} async-done(((bf16[256,6144]{1,0:T(8,128)(2,1)}), bf16[16,6144]{1,0:T(8,128)(2,1)}) %reduce-scatter.2.cloned.1.call-update) | async-done | bytes 196624 | tf_op jit(solution)/shard_map/reduce_scatter | solution.py:94
  146.7 1.0 fusion.21
  147.6 1.9 collective-permute-start
  149.6 6.5 %collective-permute-done = bf16[16,6144]{1,0:T(8,128)(2,1)S(1)} collective-permute-done((bf16[16,6144]{1,0:T(8,128)(2,1)S(1)}, bf16[16,6144]{1,0:T(8,128)(2,1)S(1)}, u32[]{:S(2)}, u32[]{:S(2)}) %collective-permute-start) | collective-permute-done | bytes 196640 | tf_op jit(solution)/shard_map/ppermute | solution.py:31
  156.1 0.2 fusion.18
  156.3 0.1 fusion.20
  156.4 0.2 broadcast_in_dim.55
  156.6 0.1 reshape.115
  156.8 0.3 convolution_convert_fusion.1
  157.1 0.3 reshape.116
  157.4 0.2 fusion.28
  157.6 0.2 select_reduce_fusion
  157.8 0.1 copy.82
  157.9 0.1 reshape.121
  158.0 0.1 fusion.6
  158.1 0.2 reshape_reshape.4
  158.3 0.4 pad_maximum_fusion
  158.7 29.5 %all_to_all.5 = bf16[1,16,4,6145]{3,2,0,1:T(4,128)(2,1)S(1)} all-to-all(bf16[1,16,4,6145]{3,2,0,1:T(4,128)(2,1)S(1)} %pad_maximum_fusion), channel_id=1, replica_groups=mesh['section'=8,'ctx'=8,'exp'=16] {'exp'}, dimensions={1} | all-to-all | bytes 1573120 | tf_op jit(solution)/shard_map/all_to_all | solution.py:39
  188.2 0.7 copy.85
  188.9 1.3 slice_bitcast_fusion
  (31 shorter events, 0.7 us)
Async XLA Ops:
  7.2 150.2 %copy-start = (bf16[1,6144,16]{1,2,0:T(8,128)(2,1)S(1)}, bf16[1,6144,16]{1,2,0:T(8,128)(2,1)}, u32[]{:S(2)}) copy-start(bf16[1,6144,16]{1,2,0:T(8,128)(2,1)} %param.16) | copy-start | bytes 589828
  7.2 59.0 %all-gather.2.cloned.1.call-start = ((), (), s32[]{:S(2)}) async-start(), calls=%async_computation.2 | async-start | bytes 1188864 | tf_op jit(solution)/shard_map/all_gather | solution.py:20
  13.2 133.5 %reduce-scatter.2.cloned.1.call-start = ((), (), s32[]{:S(2)}) async-start(), calls=%async_computation.3 | async-start | bytes 3342336 | tf_op jit(solution)/shard_map/reduce_scatter | solution.py:94
  77.7 0.7 copy-start.3
  77.7 69.0 %copy-start.1 = (bf16[1,16,6144]{2,1,0:T(8,128)(2,1)S(1)}, bf16[1,16,6144]{2,1,0:T(8,128)(2,1)}, u32[]{:S(2)}) copy-start(bf16[1,16,6144]{2,1,0:T(8,128)(2,1)} %param.14) | copy-start | bytes 589828
  77.7 78.6 %copy-start.2 = (f32[1,6144]{1,0:T(1,128)S(1)}, f32[1,6144]{1,0:T(1,128)}, u32[]{:S(2)}) copy-start(f32[1,6144]{1,0:T(1,128)} %param.15) | copy-start | bytes 73732
  147.6 8.4 %collective-permute-start = (bf16[16,6144]{1,0:T(8,128)(2,1)S(1)}, bf16[16,6144]{1,0:T(8,128)(2,1)S(1)}, u32[]{:S(2)}, u32[]{:S(2)}) collective-permute-start(bf16[16,6144]{1,0:T(8,128)(2,1)S(1)} %fusion.21), channel_id=1, source_target_pairs={{896,0},{0,128},{128,256},{256,384},{384,512},{512,640},{640,768},... | collective-permute-start | bytes 589832 | tf_op jit(solution)/shard_map/ppermute | solution.py:31
Sparse Core Ops, SparseCore 0:
  13.3 52.8 all-gather.1
  77.8 68.7 reduce-scatter.1
where the time goes:
time: 197 us
  waiting for transfers between devices  126 us (64%)
  blocking collectives  29.5 us (15%)
  between operations  14.3 us (7%)
  local copies, waits for them, and re-layouts  11.3 us (6%)
  matrix products  8.72 us (4%)
  other arithmetic  5.5 us (3%)
  starting transfers between devices  2 us (1%)
    reduce_scatter x1, waiting for transfers between devices, on_device(): lax.psum_scatter(jnp.dot(attended, projection, preferred_element_type=jnp...  67.8 us
    all_gather x1, waiting for transfers between devices, side_by_side(): lax.all_gather(both, axis, axis=dim, tiled=True)  51.3 us
    all_to_all x1, blocking collectives, in_one_piece(): lax.all_to_all(both, axis, split_axis=split_dim, concat_axis=concat_dim,...  29.5 us
    ppermute x1, waiting for transfers between devices, from_behind(): return lax.ppermute(block, axis, route)  6.49 us
    dot_general x1, matrix products, on_device(): jnp.dot(attended, projection, preferred_element_type=jnp.float32)  6.28 us
  transfers between devices with their start and end apart: 3, of which 3 were waited for; matrix products, arithmetic and copies ran while one was open for 1% of the time, Pallas kernels for 0%

commit v1 on v0

v1 whole, which is shorter than its diff:
```python
import functools

import jax
import jax.numpy as jnp
from jax import lax
from jax.experimental import pallas as pl
from jax.experimental.pallas import tpu as pltpu
from jax.sharding import PartitionSpec as P

HEAD_DIM = 128
HEAD_DEV = 4
CAP = 4
EPS = 1e-05
COLS = 256
MESH = pl.DeviceIdType.MESH
F32 = jnp.float32
BF16 = jnp.bfloat16


def iota(shape, dim):
    return lax.broadcasted_iota(jnp.int32, shape, dim)


def remote(src, dst, send_sem, recv_sem, **device):
    return pltpu.make_async_remote_copy(
        src_ref=src,
        dst_ref=dst,
        send_sem=send_sem,
        recv_sem=recv_sem,
        device_id=device,
        device_id_type=MESH,
    )


def contract(a, b, dims, **kw):
    return lax.dot_general(a, b, (dims, ((), ())), preferred_element_type=F32, **kw)


def kernel(
    sizes,
    q_hbm,
    k_hbm,
    v_hbm,
    decay_hbm,
    w_hbm,
    res_hbm,
    gain_hbm,
    router_hbm,
    ids_hbm,
    raw,
    meta,
    q_ref,
    k_ref,
    v_ref,
    decay_ref,
    res_ref,
    gain_ref,
    router_ref,
    ids_ref,
    weights,
    inner,
    attended,
    att_in,
    prod,
    state_out,
    state_in,
    scan_out,
    scan_in,
    ring_out,
    ring_in,
    shift_out,
    shift_in,
    placed,
    picks,
    squares,
    meta_out,
    load_sem,
    pair_send,
    pair_recv,
    z_send,
    z_recv,
    ring_send,
    ring_recv,
    shift_send,
    shift_recv,
    slot_send,
    slot_recv,
    meta_send,
    meta_recv,
    own_sem,
):
    n_sec, n_ctx, n_exp, length, width, cols = sizes
    n_y = n_exp // 2
    half = n_y // 2
    quarter = width // 4
    chunks = quarter // cols
    sec = lax.axis_index("section")
    ctx = lax.axis_index("ctx")
    exp = lax.axis_index("exp")
    y = exp // 2
    core = exp % 2

    def exp_at(dy, flip=0):
        there = (y + dy + n_y) % n_y
        side = 1 - core if flip else core
        return there * 2 + side

    loads = [
        pltpu.make_async_copy(src, dst, load_sem.at[i])
        for i, (src, dst) in enumerate(
            (
                (decay_hbm, decay_ref),
                (k_hbm, k_ref),
                (v_hbm, v_ref),
                (q_hbm, q_ref),
                (ids_hbm, ids_ref),
                (w_hbm, weights.at[0]),
                (res_hbm, res_ref),
                (gain_hbm, gain_ref),
                (router_hbm, router_ref),
            )
        )
    ]
    for load in loads:
        load.start()

    barrier = pltpu.get_barrier_semaphore()
    partners = 0
    for d in range(1, n_exp):
        pl.semaphore_signal(
            barrier, inc=1, device_id={"exp": (exp + d) % n_exp}, device_id_type=MESH
        )
        partners += 1
    for d in range(1, n_ctx):
        pl.semaphore_signal(
            barrier, inc=1, device_id={"ctx": (ctx + d) % n_ctx}, device_id_type=MESH
        )
        partners += 1
    if n_sec > 1:
        for d in (1, n_sec - 1):
            pl.semaphore_signal(
                barrier, inc=1, device_id={"section": (sec + d) % n_sec}, device_id_type=MESH
            )
            partners += 1

    loads[0].wait()
    lower = (iota((length, length), 0) >= iota((length, length), 1)).astype(F32)
    decay = decay_ref[...]
    b_col = -contract(lower, decay, ((1,), (1,)), precision=lax.Precision.HIGHEST)
    b_row = -contract(decay, lower, ((1,), (1,)), precision=lax.Precision.HIGHEST)
    b_last = b_col[length - 1 :, :]
    tail = jnp.exp(b_last - b_col)
    loads[1].wait()
    loads[2].wait()
    rows = HEAD_DEV * HEAD_DIM // n_ctx
    per_head = max(HEAD_DIM // rows, 1)
    for h in range(HEAD_DEV):
        at = slice(h * HEAD_DIM, (h + 1) * HEAD_DIM)
        keyed = (k_ref[:, at].astype(F32) * tail[:, h : h + 1]).astype(BF16)
        state = contract(keyed, v_ref[:, at], ((0,), (0,)))
        if n_ctx > 1:
            total = jnp.broadcast_to(b_last[:, h : h + 1], (16, HEAD_DIM))
            high = total.astype(BF16).astype(F32)
            middle = (total - high).astype(BF16).astype(F32)
            low = total - high - middle
            line = iota((16, HEAD_DIM), 0)
            log_rows = jnp.where(line == 0, high, jnp.where(line == 1, middle, low)).astype(BF16)
            for p in range(per_head):
                j = h * per_head + p
                state_out[j, 0:rows, :] = state[p * rows : (p + 1) * rows].astype(BF16)
                state_out[j, rows : rows + 16, :] = log_rows

    pl.semaphore_wait(barrier, partners)

    far_first = sorted(range(1, n_ctx), key=lambda d: -min(d, n_ctx - d))

    def z_copy(phase, d, out, into, theirs):
        peer = (ctx + d) % n_ctx
        return remote(
            out.at[peer], into.at[theirs], z_send.at[phase, d], z_recv.at[phase, d], ctx=peer
        )

    if n_ctx > 1:
        for d in far_first:
            z_copy(0, d, state_out, state_in, ctx).start()
    pair_w = remote(
        w_hbm, weights.at[1], pair_send.at[0], pair_recv.at[0], exp=exp_at(0, 1)
    )
    pair_w.start()
    if n_ctx > 1:
        state_in[ctx] = state_out[ctx]

    loads[3].wait()
    causal = iota((length, length), 0) >= iota((length, length), 1)
    for h in range(HEAD_DEV):
        at = slice(h * HEAD_DIM, (h + 1) * HEAD_DIM)
        scores = contract(q_ref[:, at], k_ref[:, at], ((1,), (1,)))
        gap = b_col[:, h : h + 1] - b_row[h : h + 1, :]
        mix = jnp.where(causal, scores * jnp.exp(jnp.minimum(gap, 0.0)), 0.0).astype(BF16)
        inner[:, at] = jnp.dot(mix, v_ref[:, at], preferred_element_type=F32)

    tok = ids_ref.shape[0]
    loads[4].wait()
    ids = ids_ref[...]
    first_id, second_id = ids[:, 0:1], ids[:, 1:2]
    experts = iota((tok, n_exp), 1)
    is_first = (first_id == experts).astype(F32)
    is_second = (second_id == experts).astype(F32)
    match = is_first + is_second
    earlier = (iota((tok, tok), 0) > iota((tok, tok), 1)).astype(F32)
    rank = jnp.dot(earlier.astype(BF16), match.astype(BF16), preferred_element_type=F32)
    code = jnp.where(match > 0.5, rank, -1.0)
    code4 = jnp.concatenate([code] * 4, axis=0)
    slot_rows = n_exp * 16
    spread = (iota((slot_rows, n_exp), 0) // 16 == iota((slot_rows, n_exp), 1)).astype(BF16)
    codes = contract(spread, code4.astype(BF16), ((1,), (1,)))
    line = iota((slot_rows, 4 * tok), 0) % 16
    part = iota((slot_rows, 4 * tok), 1) // tok
    picks[...] = jnp.where(
        jnp.logical_and(codes == (line % CAP).astype(F32), part == line // CAP), 1.0, 0.0
    ).astype(BF16)

    if n_ctx > 1:
        for d in far_first:
            z_copy(0, d, state_out, state_in, (ctx - d + n_ctx) % n_ctx).wait_recv()
        carried = jnp.zeros((rows, HEAD_DIM), F32)
        for n in range(n_ctx):
            scan_out[n] = carried.astype(BF16)
            if n < n_ctx - 1:
                logs = state_in[n, rows : rows + 16, :].astype(F32)
                total = logs[0:1] + logs[1:2] + logs[2:3]
                carried = jnp.exp(total) * carried + state_in[n, 0:rows, :].astype(F32)
        for d in far_first:
            z_copy(1, d, scan_out, scan_in, ctx).start()
        scan_in[ctx] = scan_out[ctx]
        for d in far_first:
            z_copy(1, d, scan_out, scan_in, (ctx - d + n_ctx) % n_ctx).wait_recv()

    grow = jnp.exp(b_col)
    for h in range(HEAD_DEV):
        at = slice(h * HEAD_DIM, (h + 1) * HEAD_DIM)
        whole = inner[:, at]
        if n_ctx > 1:
            pieces = [scan_in[h * per_head + p] for p in range(per_head)]
            incoming = jnp.concatenate(pieces, axis=0) if per_head > 1 else pieces[0]
            carried = jnp.dot(q_ref[:, at], incoming, preferred_element_type=F32)
            whole = whole + grow[:, h : h + 1] * carried
        split = whole.astype(BF16).reshape(n_y, 2, tok, HEAD_DIM)
        for c in range(2):
            attended[c, :, at] = split[:, c].reshape(n_y * tok, HEAD_DIM)
    pair_a = remote(
        attended.at[1 - core], att_in, pair_send.at[1], pair_recv.at[1], exp=exp_at(0, 1)
    )
    pair_a.start()
    loads[5].wait()
    loads[6].wait()
    pair_w.wait_recv()
    pair_a.wait_recv()

    right, left = exp_at(1), exp_at(-1)
    span = 2 * tok

    def ring_copy(way, step, i):
        src, dst = ring_out.at[way, step, i], ring_in.at[way, step, i]
        if step == 0:
            src, dst = src.at[pl.ds(way * span, span)], dst.at[pl.ds(way * span, span)]
        return remote(
            src,
            dst,
            ring_send.at[way, step, i],
            ring_recv.at[way, step, i],
            exp=left if way else right,
        )

    def dest(way, step):
        away = half - step
        return (y - away + n_y) % n_y if way else (y + away) % n_y

    @pl.loop(0, chunks)
    def _(i):
        mine, theirs = attended[core], att_in[...]
        for c in range(4):
            at = pl.ds(pl.multiple_of(c * quarter + i * cols, 128), cols)
            term = jnp.dot(mine, weights[0, :, at], preferred_element_type=F32)
            term = term + jnp.dot(theirs, weights[1, :, at], preferred_element_type=F32)
            prod[i, :, c * tok : (c + 1) * tok, :] = term.reshape(n_y, tok, cols)
        for way in range(2):
            part = slice(way * span, (way + 1) * span)
            ring_out[way, 0, i, part, :] = prod[i, dest(way, 0), part, :].astype(BF16)
            ring_copy(way, 0, i).start()

    for step in range(1, half):

        @pl.loop(0, chunks)
        def _(i, step=step):
            for way in range(2):
                ring_copy(way, step - 1, i).wait_recv()
                to = dest(way, step)
                if step == 1:
                    for p in range(2):
                        part = slice(p * span, (p + 1) * span)
                        total = prod[i, to, part, :]
                        if p == way:
                            total = total + ring_in[way, 0, i, part, :].astype(F32)
                        ring_out[way, 1, i, part, :] = total.astype(BF16)
                else:
                    total = prod[i, to] + ring_in[way, step - 1, i].astype(F32)
                    ring_out[way, step, i] = total.astype(BF16)
                ring_copy(way, step, i).start()

    def shift_copy(i):
        return remote(
            shift_out.at[i],
            shift_in.at[i],
            shift_send.at[i],
            shift_recv.at[i],
            section=(sec + 1) % n_sec,
        )

    def slot_copy(i, dy, flip, sender):
        peer = exp_at(dy, flip)
        k = dy * 2 + flip
        return remote(
            placed.at[i, peer], raw.at[sender, i], slot_send.at[i, k], slot_recv.at[i, k], exp=peer
        )

    def own_copy(i):
        return pltpu.make_async_copy(placed.at[i, exp], raw.at[exp, i], own_sem.at[i])

    order = sorted(range(1, n_y), key=lambda d: -min(d, n_y - d)) + [0]
    others = [(dy, flip) for dy in order for flip in (0, 1) if (dy, flip) != (0, 0)]

    squares[...] = jnp.zeros_like(squares)

    @pl.loop(0, chunks + 2)
    def _(i):
        @pl.when(i < chunks)
        def _():
            ring_copy(0, half - 1, i).wait_recv()
            ring_copy(1, half - 1, i).wait_recv()
            for c in range(4):
                part = slice(c * tok, (c + 1) * tok)
                at = pl.ds(pl.multiple_of(c * quarter + i * cols, 128), cols)
                total = prod[i, y, part, :]
                for way in range(2):
                    if half > 1 or way == c // 2:
                        total = total + ring_in[way, half - 1, i, part, :].astype(F32)
                total = total + res_ref[:, at].astype(F32)
                shift_out[i, part, :] = total.astype(BF16)
            if n_sec > 1:
                shift_copy(i).start()
            else:
                shift_in[i] = shift_out[i]

        @pl.when(i >= 2)
        def _():
            now = i - 2
            if n_sec > 1:
                shift_copy(now).wait_recv()
            rows_in = shift_in[now]
            wide = rows_in.astype(F32)
            squares[...] += jnp.sum(wide * wide, axis=-1, keepdims=True)
            slots = jnp.dot(picks[...], rows_in, preferred_element_type=F32)
            placed[now] = slots.astype(BF16).reshape(n_exp, 16, cols)
            for dy, flip in others:
                slot_copy(now, dy, flip, exp).start()
            own_copy(now).start()

    loads[7].wait()
    loads[8].wait()
    total = squares[0:tok, 0:1]
    for c in range(1, 4):
        total = total + squares[c * tok : (c + 1) * tok, 0:1]
    factor = lax.rsqrt(total / width + EPS)
    logits = jnp.zeros((tok, n_exp), F32)
    for c in range(4):
        for i in range(chunks):
            at = slice(c * quarter + i * cols, c * quarter + (i + 1) * cols)
            wide = shift_in[i, c * tok : (c + 1) * tok, :].astype(F32)
            normed = (wide * factor * gain_ref[:, at]).astype(BF16)
            logits = logits + jnp.dot(normed, router_ref[at, :], preferred_element_type=F32)
    picked0 = jnp.sum(logits * is_first, axis=-1, keepdims=True)
    picked1 = jnp.sum(logits * is_second, axis=-1, keepdims=True)
    gate0 = 1.0 / (1.0 + jnp.exp(picked1 - picked0))
    gate1 = 1.0 - gate0
    info_rows = n_exp * 2 * CAP
    spread8 = (iota((info_rows, n_exp), 0) // 8 == iota((info_rows, n_exp), 1)).astype(BF16)
    codes8 = contract(spread8, code.astype(BF16), ((1,), (1,)))
    first8 = contract(spread8, is_first.astype(BF16), ((1,), (1,)))
    diagonal = (iota((tok, tok), 0) == iota((tok, tok), 1)).astype(F32)

    def lying(column):
        return jnp.sum(diagonal * column, axis=0, keepdims=True)

    line8 = iota((info_rows, tok), 0) % 8
    gates = jnp.where(first8 > 0.5, lying(gate0), lying(gate1))
    info = jnp.where(line8 < CAP, lying(factor), gates)
    info = jnp.where(codes8 == (line8 % CAP).astype(F32), info, 0.0)
    info = jnp.sum(info, axis=-1, keepdims=True)
    meta_out[...] = jnp.broadcast_to(info, (info_rows, 128)).reshape(n_exp, 8, 128)

    def meta_copy(dy, flip, sender):
        peer = exp_at(dy, flip)
        k = dy * 2 + flip
        return remote(
            meta_out.at[peer], meta.at[sender], meta_send.at[k], meta_recv.at[k], exp=peer
        )

    own_meta = pltpu.make_async_copy(meta_out.at[exp], meta.at[exp], own_sem.at[chunks])
    for dy, flip in others:
        meta_copy(dy, flip, exp).start()
    own_meta.start()

    pair_w.wait_send()
    pair_a.wait_send()
    for d in far_first:
        for phase, (out, into) in enumerate(((state_out, state_in), (scan_out, scan_in))):
            z_copy(phase, d, out, into, ctx).wait_send()

    @pl.loop(0, chunks)
    def _(i):
        for way in range(2):
            for step in range(half):
                ring_copy(way, step, i).wait_send()
        if n_sec > 1:
            shift_copy(i).wait_send()
        own_copy(i).wait()
        for dy, flip in others:
            sender = exp_at(-dy, flip)
            slot_copy(i, dy, flip, exp).wait_send()
            slot_copy(i, dy, flip, sender).wait_recv()

    own_meta.wait()
    for dy, flip in others:
        meta_copy(dy, flip, exp).wait_send()
        meta_copy(dy, flip, exp_at(-dy, flip)).wait_recv()


def on_device(
    sizes, queries, keys_in, values, decay_rate, out_weight, residual, norm_gain, router, expert_ids
):
    n_sec, n_ctx, n_exp = sizes
    length, inner_width = queries.shape[1:]
    width = out_weight.shape[-1]
    tok = residual.shape[1]
    n_y = n_exp // 2
    half = n_y // 2
    quarter = width // 4
    cols = min(COLS, quarter // 2)
    chunks = quarter // cols
    rows = HEAD_DEV * HEAD_DIM // n_ctx
    any_space = pl.BlockSpec(memory_space=pl.ANY)
    dma = pltpu.SemaphoreType.DMA
    raw, meta = pl.pallas_call(
        functools.partial(kernel, (n_sec, n_ctx, n_exp, length, width, cols)),
        out_shape=(
            jax.ShapeDtypeStruct((n_exp, chunks, 16, cols), BF16),
            jax.ShapeDtypeStruct((n_exp, 8, 128), F32),
        ),
        in_specs=[any_space] * 9,
        out_specs=(any_space, any_space),
        scratch_shapes=[
            pltpu.VMEM((length, inner_width), BF16),
            pltpu.VMEM((length, inner_width), BF16),
            pltpu.VMEM((length, inner_width), BF16),
            pltpu.VMEM((HEAD_DEV, length), F32),
            pltpu.VMEM((tok, width), BF16),
            pltpu.VMEM((1, width), F32),
            pltpu.VMEM((width, n_exp), BF16),
            pltpu.VMEM((tok, 2), jnp.int32),
            pltpu.VMEM((2, inner_width, width), BF16),
            pltpu.VMEM((length, inner_width), F32),
            pltpu.VMEM((2, n_y * tok, inner_width), BF16),
            pltpu.VMEM((n_y * tok, inner_width), BF16),
            pltpu.VMEM((chunks, n_y, 4 * tok, cols), F32),
            pltpu.VMEM((n_ctx, rows + 16, HEAD_DIM), BF16),
            pltpu.VMEM((n_ctx, rows + 16, HEAD_DIM), BF16),
            pltpu.VMEM((n_ctx, rows, HEAD_DIM), BF16),
            pltpu.VMEM((n_ctx, rows, HEAD_DIM), BF16),
            pltpu.VMEM((2, half, chunks, 4 * tok, cols), BF16),
            pltpu.VMEM((2, half, chunks, 4 * tok, cols), BF16),
            pltpu.VMEM((chunks, 4 * tok, cols), BF16),
            pltpu.VMEM((chunks, 4 * tok, cols), BF16),
            pltpu.VMEM((chunks, n_exp, 16, cols), BF16),
            pltpu.VMEM((n_exp * 16, 4 * tok), BF16),
            pltpu.VMEM((4 * tok, 128), F32),
            pltpu.VMEM((n_exp, 8, 128), F32),
            dma((9,)),
            dma((2,)),
            dma((2,)),
            dma((2, n_ctx)),
            dma((2, n_ctx)),
            dma((2, half, chunks)),
            dma((2, half, chunks)),
            dma((chunks,)),
            dma((chunks,)),
            dma((chunks, n_exp)),
            dma((chunks, n_exp)),
            dma((n_exp,)),
            dma((n_exp,)),
            dma((chunks + 1,)),
        ],
        compiler_params=pltpu.CompilerParams(
            collective_id=0, has_side_effects=True, vmem_limit_bytes=56 * 2**20
        ),
    )(
        queries[0],
        keys_in[0],
        values[0],
        decay_rate[0],
        out_weight[0],
        residual[0],
        norm_gain,
        router[0],
        expert_ids[0],
    )
    factor = meta[:, 0:CAP, 0]
    gates = meta[:, CAP : 2 * CAP, 0].astype(BF16)
    rows_in = raw.reshape(n_exp, chunks, 4, CAP, cols).astype(F32)
    gain = norm_gain[0].reshape(4, chunks, cols).transpose(1, 0, 2)
    normed = (
        rows_in * factor[:, None, None, :, None] * gain[None, :, :, None, :]
    ).astype(BF16)
    normed = normed.transpose(0, 3, 2, 1, 4).reshape(n_exp, CAP, width)
    return (normed[None, None, None], gates[None, None, None])


def solution(mesh):
    sizes = tuple(mesh.shape[a] for a in ("section", "ctx", "exp"))
    placed = (
        P("section", "ctx", "exp"),
        P("section", "ctx", "exp"),
        P("section", "ctx", "exp"),
        P("section", "exp", "ctx"),
        P("section", "exp", None),
        P("section", ("ctx", "exp"), None),
        P("section", None),
        P("section", None, None),
        P("section", ("ctx", "exp"), None),
    )
    return jax.shard_map(
        functools.partial(on_device, sizes),
        mesh=mesh,
        in_specs=placed,
        out_specs=(
            P("section", "ctx", "exp", None, None, None),
            P("section", "ctx", "exp", None, None),
        ),
        check_vma=False,
    )
```

time: 197 us -> 92.2 us (0.47)
  waiting for transfers between devices: 126 us -> 0 us
  Pallas kernels: 0 us -> 78 us
  blocking collectives: 29.5 us -> 0 us
  between operations: 14.3 us -> 0.68 us
  matrix products: 8.72 us -> 0 us
  other arithmetic: 5.5 us -> 2.35 us
  starting transfers between devices: 2 us -> 0 us
    pallas_call x0 -> x1, Pallas kernels: none -> 78 us  [on_device(): pl.pallas_call(functools.partial(kernel, (n_sec, n_ctx, n_exp, length, wi...]
    reduce_scatter x1 -> x0, waiting for transfers between devices: 67.8 us -> none  [on_device(): lax.psum_scatter(jnp.dot(attended, projection, preferred_element_type=jnp...]
    all_gather x1 -> x0, waiting for transfers between devices: 51.3 us -> none  [side_by_side(): lax.all_gather(both, axis, axis=dim, tiled=True)]
    all_to_all x1 -> x0, blocking collectives: 29.5 us -> none  [in_one_piece(): lax.all_to_all(both, axis, split_axis=split_dim, concat_axis=concat_dim,...]
    dot_general x8 -> x0, matrix products: 8.72 us -> none  [the longest x1 6.28 us: on_device(): jnp.dot(attended, projection, preferred_element_type=jnp.float32)]
    ppermute x1 -> x0, waiting for transfers between devices: 6.49 us -> none  [from_behind(): return lax.ppermute(block, axis, route)]
    unnamed x12 -> x3, local copies, waits for them, and re-layouts: 0.97 us -> 4.37 us
    another operation x8 -> x2, local copies, waits for them, and re-layouts: 3.57 us -> 0.86 us  [the longest x1 0.85 us: on_device(): return (normed[None, None, None], gates[None, None, None])]
  transfers between devices with their start and end apart: 3 -> 0, of which waited for: 3 -> 0; matrix products, arithmetic and copies ran while one was open for 1% -> 0% of each run, Pallas kernels for 0% -> 0%
where the time goes in v1:
time: 92.2 us; the launch traced here: 91.8 us
  Pallas kernels  78 us (85%)
  local copies, waits for them, and re-layouts  10.7 us (12%)
  other arithmetic  2.35 us (3%)
    pallas_call x1, Pallas kernels, on_device(): pl.pallas_call(functools.partial(kernel, (n_sec, n_ctx, n_exp, length, wi...  78 us
    unnamed x3, local copies, waits for them, and re-layouts  4.37 us

profile of v1, /device:TPU:1, one launch (start us, length us, event | category | flops | bytes accessed | tf_op | source)
XLA Modules:
  0.0 91.8 jit_solution(5446117402231524035)
XLA Ops:
  0.6 1.4 %copy.19.ids_hbm = s32[16,2]{1,0:T(8,128)} copy(s32[16,2]{0,1:T(2,128)} %bitcast.26) | data formatting | bytes 256 | tf_op jit(solution)/shard_map/squeeze | solution.py:515
  2.0 0.5 broadcast.4
  2.5 1.4 %reduce.3 = f32[6144]{0:T(1024)S(1)} reduce(f32[1,6144]{1,0:T(1,128)} %gain_hbm.1, f32[]{:T(128)} %broadcast.4), dimensions={0}, to_apply=%param.15.reduce_sub_computation.3 | reduce | bytes 49156 | tf_op args[6]
  4.0 2.4 %copy.18 = bf16[1,6144,16]{2,1,0:T(8,128)(2,1)} copy(bf16[1,6144,16]{1,2,0:T(8,128)(2,1)} %param.16) | data formatting | bytes 393216 | tf_op args[7]
  6.3 78.0 %shard_map.104 = (bf16[16,6,16,256]{3,2,1,0:T(8,128)(2,1)}, f32[16,8,128]{2,1,0:T(8,128)}) custom-call(bf16[256,512]{1,0:T(8,128)(2,1)} %bitcast.19, bf16[256,512]{1,0:T(8,128)(2,1)} %bitcast.20, bf16[256,512]{1,0:T(8,128)(2,1)} %bitcast.21, f32[4,256]{1,0:T(4,128)} %bitcast.25, bf16[512,6144]{1,0:T(8,128)(2,1)} %bitcast.17, bf16[16,6144]{1,0:T(8,128)(2,1)} %bitcast.22, ...), custom_call_target="tpu_custom_call" | custom-call | tf_op jit(solution)/shard_map/pallas_call | solution.py:454
  84.4 0.8 slice.11
  85.2 0.8 slice.7
  86.1 0.1 copy.20
  86.2 0.7 copy.22
  86.8 1.7 %reshape.20 = f32[16,6,4,4,256]{4,3,2,1,0:T(4,128)S(1)} reshape(bf16[16,6,16,256]{3,2,1,0:T(8,128)(2,1)} %get-tuple-element.4) | data formatting | bytes 2359296 | tf_op jit(solution)/shard_map/convert_element_type | solution.py:519
  88.5 0.9 fusion.2
  89.4 0.8 broadcast_in_dim_reshape.3
  90.3 1.5 %copy.23 = bf16[1,1,1,16,4,6144]{5,4,3,2,1,0:T(4,128)(2,1)} copy(bf16[1,1,1,16,4,6144]{5,3,4,2,1,0:T(8,128)(2,1)S(1)} %broadcast_in_dim_reshape.3) | data formatting | bytes 1572864
  (1 shorter events, 0.0 us)

commit v2 on v1

v2 whole, which is shorter than its diff:
```python
import functools

import jax
import jax.numpy as jnp
from jax import lax
from jax.experimental import pallas as pl
from jax.experimental.pallas import tpu as pltpu
from jax.sharding import PartitionSpec as P

HEAD_DIM = 128
HEAD_DEV = 4
CAP = 4
EPS = 1e-05
COLS = 1024
RAW = 2
VMEM_MIB = 36
MESH = pl.DeviceIdType.MESH
F32 = jnp.float32
BF16 = jnp.bfloat16


def iota(shape, dim):
    return lax.broadcasted_iota(jnp.int32, shape, dim)


def remote(src, dst, send_sem, recv_sem, **device):
    return pltpu.make_async_remote_copy(
        src_ref=src,
        dst_ref=dst,
        send_sem=send_sem,
        recv_sem=recv_sem,
        device_id=device,
        device_id_type=MESH,
    )


def contract(a, b, dims, **kw):
    return lax.dot_general(a, b, (dims, ((), ())), preferred_element_type=F32, **kw)


def kernel(
    sizes,
    q_hbm,
    k_hbm,
    v_hbm,
    decay_hbm,
    w_hbm,
    res_hbm,
    gain_hbm,
    router_hbm,
    ids_hbm,
    rows_out,
    meta_in,
    q_ref,
    k_ref,
    v_ref,
    decay_ref,
    res_ref,
    gain_ref,
    router_ref,
    ids_ref,
    weights,
    inner,
    attended,
    att_in,
    prod,
    state_out,
    state_in,
    scan_out,
    scan_in,
    ring_out,
    ring_in,
    shift_out,
    shift_in,
    placed,
    picks,
    squares,
    meta_out,
    load_sem,
    pair_send,
    pair_recv,
    z_send,
    z_recv,
    ring_send,
    ring_recv,
    half_send,
    half_recv,
    shift_send,
    shift_recv,
    slot_send,
    slot_recv,
    meta_send,
    meta_recv,
    own_sem,
):
    n_sec, n_ctx, n_exp, length, width, cols = sizes
    n_y = n_exp // 2
    half = n_y // 2
    chunks = width // cols
    tok = length // n_exp
    sec = lax.axis_index("section")
    ctx = lax.axis_index("ctx")
    exp = lax.axis_index("exp")
    y = exp // 2
    core = exp % 2

    def exp_at(dy, flip=0):
        there = (y + dy + n_y) % n_y
        side = 1 - core if flip else core
        return there * 2 + side

    loads = [
        pltpu.make_async_copy(src, dst, load_sem.at[i])
        for i, (src, dst) in enumerate(
            (
                (decay_hbm, decay_ref),
                (k_hbm, k_ref),
                (v_hbm, v_ref),
                (q_hbm, q_ref),
                (ids_hbm, ids_ref),
                (w_hbm, weights.at[0]),
                (res_hbm, res_ref),
                (gain_hbm, gain_ref),
                (router_hbm, router_ref),
            )
        )
    ]
    for load in loads:
        load.start()

    barrier = pltpu.get_barrier_semaphore()
    partners = 0
    for d in range(1, n_exp):
        pl.semaphore_signal(
            barrier, inc=1, device_id={"exp": (exp + d) % n_exp}, device_id_type=MESH
        )
        partners += 1
    for d in range(1, n_ctx):
        pl.semaphore_signal(
            barrier, inc=1, device_id={"ctx": (ctx + d) % n_ctx}, device_id_type=MESH
        )
        partners += 1
    if n_sec > 1:
        for d in (1, n_sec - 1):
            pl.semaphore_signal(
                barrier, inc=1, device_id={"section": (sec + d) % n_sec}, device_id_type=MESH
            )
            partners += 1

    loads[0].wait()
    lower = (iota((length, length), 0) >= iota((length, length), 1)).astype(BF16)
    rest = -decay_ref[...]
    b_col = jnp.zeros((length, HEAD_DEV), F32)
    b_row = jnp.zeros((HEAD_DEV, length), F32)
    for _ in range(3):
        part = rest.astype(BF16)
        rest = rest - part.astype(F32)
        b_col = b_col + contract(lower, part, ((1,), (1,)))
        b_row = b_row + contract(part, lower, ((1,), (1,)))
    b_last = b_col[length - 1 :, :]
    tail = jnp.exp(b_last - b_col)
    loads[1].wait()
    loads[2].wait()
    rows = HEAD_DEV * HEAD_DIM // n_ctx
    per_head = max(HEAD_DIM // rows, 1)
    for h in range(HEAD_DEV):
        at = slice(h * HEAD_DIM, (h + 1) * HEAD_DIM)
        keyed = (k_ref[:, at].astype(F32) * tail[:, h : h + 1]).astype(BF16)
        state = contract(keyed, v_ref[:, at], ((0,), (0,)))
        if n_ctx > 1:
            total = jnp.broadcast_to(b_last[:, h : h + 1], (16, HEAD_DIM))
            high = total.astype(BF16).astype(F32)
            middle = (total - high).astype(BF16).astype(F32)
            low = total - high - middle
            line = iota((16, HEAD_DIM), 0)
            log_rows = jnp.where(line == 0, high, jnp.where(line == 1, middle, low)).astype(BF16)
            for p in range(per_head):
                j = h * per_head + p
                state_out[j, 0:rows, :] = state[p * rows : (p + 1) * rows].astype(BF16)
                state_out[j, rows : rows + 16, :] = log_rows

    pl.semaphore_wait(barrier, partners)

    far_first = sorted(range(1, n_ctx), key=lambda d: -min(d, n_ctx - d))

    def z_copy(phase, d, out, into, theirs):
        peer = (ctx + d) % n_ctx
        return remote(
            out.at[peer], into.at[theirs], z_send.at[phase, d], z_recv.at[phase, d], ctx=peer
        )

    if n_ctx > 1:
        for d in far_first:
            z_copy(0, d, state_out, state_in, ctx).start()
    def columns(i):
        return pl.ds(pl.multiple_of(i * cols, 128), cols)

    def pair_w(i):
        return remote(
            w_hbm.at[:, columns(i)],
            weights.at[1, :, columns(i)],
            pair_send.at[i],
            pair_recv.at[i],
            exp=exp_at(0, 1),
        )

    for i in range(chunks):
        pair_w(i).start()
    if n_ctx > 1:
        state_in[ctx] = state_out[ctx]

    loads[3].wait()
    causal = iota((length, length), 0) >= iota((length, length), 1)
    for h in range(HEAD_DEV):
        at = slice(h * HEAD_DIM, (h + 1) * HEAD_DIM)
        scores = contract(q_ref[:, at], k_ref[:, at], ((1,), (1,)))
        gap = b_col[:, h : h + 1] - b_row[h : h + 1, :]
        mix = jnp.where(causal, scores * jnp.exp(jnp.minimum(gap, 0.0)), 0.0).astype(BF16)
        inner[:, at] = jnp.dot(mix, v_ref[:, at], preferred_element_type=F32)

    loads[4].wait()
    ids = ids_ref[...]
    experts = iota((n_exp, tok), 0)
    is_first = (ids[0:1] == experts).astype(F32)
    match = is_first + (ids[1:2] == experts).astype(F32)
    earlier = (iota((tok, tok), 0) < iota((tok, tok), 1)).astype(BF16)
    rank = jnp.dot(match.astype(BF16), earlier, preferred_element_type=F32)
    code = jnp.where(match > 0.5, rank, -1.0).astype(BF16)
    slot_rows = n_exp * 8
    spread = (iota((slot_rows, n_exp), 0) // 8 == iota((slot_rows, n_exp), 1)).astype(BF16)
    codes = jnp.dot(spread, code, preferred_element_type=F32)
    line = iota((slot_rows, tok), 0) % 8
    picks[...] = (codes == line.astype(F32)).astype(BF16)

    if n_ctx > 1:
        for d in far_first:
            z_copy(0, d, state_out, state_in, (ctx - d + n_ctx) % n_ctx).wait_recv()
        carried = jnp.zeros((rows, HEAD_DIM), F32)
        for n in range(n_ctx):
            scan_out[n] = carried.astype(BF16)
            if n < n_ctx - 1:
                logs = state_in[n, rows : rows + 16, :].astype(F32)
                total = logs[0:1] + logs[1:2] + logs[2:3]
                carried = jnp.exp(total) * carried + state_in[n, 0:rows, :].astype(F32)
        for d in far_first:
            z_copy(1, d, scan_out, scan_in, ctx).start()
        scan_in[ctx] = scan_out[ctx]
        for d in far_first:
            z_copy(1, d, scan_out, scan_in, (ctx - d + n_ctx) % n_ctx).wait_recv()

    grow = jnp.exp(b_col)
    for h in range(HEAD_DEV):
        at = slice(h * HEAD_DIM, (h + 1) * HEAD_DIM)
        whole = inner[:, at]
        if n_ctx > 1:
            pieces = [scan_in[h * per_head + p] for p in range(per_head)]
            incoming = jnp.concatenate(pieces, axis=0) if per_head > 1 else pieces[0]
            carried = jnp.dot(q_ref[:, at], incoming, preferred_element_type=F32)
            whole = whole + grow[:, h : h + 1] * carried
        split = whole.astype(BF16).reshape(n_y, 2, tok, HEAD_DIM)
        for c in range(2):
            attended[c, :, at] = split[:, c].reshape(n_y * tok, HEAD_DIM)
    pair_a = remote(
        attended.at[1 - core], att_in, pair_send.at[chunks], pair_recv.at[chunks], exp=exp_at(0, 1)
    )
    pair_a.start()
    loads[5].wait()
    loads[6].wait()

    right, left = exp_at(1), exp_at(-1)
    span = cols // 2

    def ring_copy(way, step, i):
        return remote(
            ring_out.at[way, step, i],
            ring_in.at[way, step, i],
            ring_send.at[way, step, i],
            ring_recv.at[way, step, i],
            exp=left if way else right,
        )

    def half_copy(way, step, i, p):
        part = pl.ds(p * span, span)
        return remote(
            ring_out.at[way, step, i, :, part],
            ring_in.at[way, step, i, :, part],
            half_send.at[way, step, i, p],
            half_recv.at[way, step, i, p],
            exp=left if way else right,
        )

    def arrived(way, step, i):
        if step > 1:
            ring_copy(way, step, i).wait_recv()
        else:
            for p in range(2):
                if step == 1 or p == way:
                    half_copy(way, step, i, p).wait_recv()

    def dest(way, step):
        away = half - step
        return (y - away + n_y) % n_y if way else (y + away) % n_y

    def first_send(way, step, i, p):
        part = slice(p * span, (p + 1) * span)
        ring_out[way, step, i, :, part] = prod[i, dest(way, step), :, part].astype(BF16)
        half_copy(way, step, i, p).start()

    def pass_on(step, i):
        for way in range(2):
            arrived(way, step - 1, i)
            total = prod[i, dest(way, step)] + ring_in[way, step - 1, i].astype(F32)
            ring_out[way, step, i] = total.astype(BF16)
            ring_copy(way, step, i).start()

    lag = 2 if half > 1 else 0

    @pl.loop(0, chunks + lag)
    def _(i):
        @pl.when(i < chunks)
        def _():
            at = columns(i)
            term = jnp.dot(attended[core], weights[0, :, at], preferred_element_type=F32)

            @pl.when(i == 0)
            def _():
                pair_a.wait_recv()

            pair_w(i).wait_recv()
            term = term + jnp.dot(att_in[...], weights[1, :, at], preferred_element_type=F32)
            prod[i] = term.reshape(n_y, tok, cols)
            for way in range(2):
                first_send(way, 0, i, way)
            if half > 1:
                for way in range(2):
                    first_send(way, 1, i, 1 - way)

        if half > 1:

            @pl.when(i >= lag)
            def _():
                now = i - lag
                for way in range(2):
                    part = slice(way * span, (way + 1) * span)
                    half_copy(way, 0, now, way).wait_recv()
                    total = prod[now, dest(way, 1), :, part]
                    total = total + ring_in[way, 0, now, :, part].astype(F32)
                    ring_out[way, 1, now, :, part] = total.astype(BF16)
                    half_copy(way, 1, now, way).start()

    for step in range(2, half):

        @pl.loop(0, chunks)
        def _(i, step=step):
            pass_on(step, i)

    def shift_copy(i):
        return remote(
            shift_out.at[i],
            shift_in.at[i],
            shift_send.at[i],
            shift_recv.at[i],
            section=(sec + 1) % n_sec,
        )

    def slot_copy(i, dy, flip, sender):
        peer = exp_at(dy, flip)
        k = dy * 2 + flip
        return remote(
            placed.at[i, peer],
            rows_out.at[sender, :, columns(i)],
            slot_send.at[i, k],
            slot_recv.at[i, k],
            exp=peer,
        )

    def own_copy(i):
        return pltpu.make_async_copy(
            placed.at[i, exp], rows_out.at[exp, :, columns(i)], own_sem.at[i]
        )

    order = sorted(range(1, n_y), key=lambda d: -min(d, n_y - d)) + [0]
    others = [(dy, flip) for dy in order for flip in (0, 1) if (dy, flip) != (0, 0)]

    def place(i):
        slots = jnp.dot(picks[...], shift_in[i], preferred_element_type=F32)
        placed[i] = slots.reshape(n_exp, 8, cols)[:, 0:CAP].astype(BF16)
        for dy, flip in others:
            slot_copy(i, dy, flip, exp).start()
        own_copy(i).start()

    squares[...] = jnp.zeros_like(squares)

    def add_squares(i):
        if n_sec > 1:
            shift_copy(i).wait_recv()
        wide = shift_in[i].astype(F32)
        squares[...] += jnp.sum(wide * wide, axis=-1, keepdims=True)

    @pl.loop(0, chunks)
    def _(i):
        arrived(0, half - 1, i)
        arrived(1, half - 1, i)
        at = columns(i)
        for p in range(2):
            part = slice(p * span, (p + 1) * span)
            total = prod[i, y, :, part]
            for way in range(2):
                if half > 1 or way == p:
                    total = total + ring_in[way, half - 1, i, :, part].astype(F32)
            wide = res_ref[:, pl.ds(pl.multiple_of(i * cols + p * span, 128), span)]
            shift_out[i, :, part] = (total + wide.astype(F32)).astype(BF16)
        if n_sec > 1:
            shift_copy(i).start()
        else:
            shift_in[i] = shift_out[i]

        @pl.when(jnp.logical_and(i >= 2, i < RAW + 2))
        def _():
            now = i - 2
            add_squares(now)
            place(now)

    @pl.loop(RAW, chunks)
    def _(i):
        add_squares(i)

    loads[7].wait()
    loads[8].wait()
    factor = lax.rsqrt(squares[:, 0:1] / width + EPS)
    logits = jnp.zeros((n_exp, tok), F32)
    for i in range(chunks):
        at = slice(i * cols, (i + 1) * cols)
        normed = (shift_in[i].astype(F32) * factor * gain_ref[:, at]).astype(BF16)
        if i >= RAW:
            shift_in[i] = normed
        logits = logits + contract(router_ref[:, at], normed, ((1,), (1,)))
    picked0 = jnp.sum(logits * is_first, axis=0, keepdims=True)
    picked1 = jnp.sum(logits * (match - is_first), axis=0, keepdims=True)
    gate0 = 1.0 / (1.0 + jnp.exp(picked1 - picked0))
    gate1 = 1.0 - gate0
    diagonal = (iota((tok, tok), 0) == iota((tok, tok), 1)).astype(F32)
    lying = jnp.sum(diagonal * factor, axis=0, keepdims=True)
    first8 = jnp.dot(spread, is_first.astype(BF16), preferred_element_type=F32)
    info = jnp.where(line < CAP, lying, jnp.where(first8 > 0.5, gate0, gate1))
    info = jnp.where(codes == (line % CAP).astype(F32), info, 0.0)
    info = jnp.sum(info, axis=-1, keepdims=True)
    meta_out[...] = jnp.broadcast_to(info, (slot_rows, 128)).reshape(n_exp, 8, 128)

    def meta_copy(dy, flip, sender):
        peer = exp_at(dy, flip)
        k = dy * 2 + flip
        return remote(
            meta_out.at[peer], meta_in.at[sender], meta_send.at[k], meta_recv.at[k], exp=peer
        )

    for dy, flip in others:
        meta_copy(dy, flip, exp).start()
    own_meta = pltpu.make_async_copy(meta_out.at[exp], meta_in.at[exp], own_sem.at[chunks])
    own_meta.start()

    @pl.loop(RAW, chunks)
    def _(i):
        place(i)

    pair_a.wait_send()
    for d in far_first:
        for phase, (out, into) in enumerate(((state_out, state_in), (scan_out, scan_in))):
            z_copy(phase, d, out, into, ctx).wait_send()

    @pl.loop(0, chunks)
    def _(i):
        pair_w(i).wait_send()
        for way in range(2):
            for step in range(half):
                if step > 1:
                    ring_copy(way, step, i).wait_send()
                else:
                    for p in range(2):
                        if step == 1 or p == way:
                            half_copy(way, step, i, p).wait_send()
        if n_sec > 1:
            shift_copy(i).wait_send()
        own_copy(i).wait()
        for dy, flip in others:
            slot_copy(i, dy, flip, exp).wait_send()
            slot_copy(i, dy, flip, exp_at(-dy, flip)).wait_recv()

    own_meta.wait()
    for dy, flip in others:
        meta_copy(dy, flip, exp).wait_send()
        meta_copy(dy, flip, exp_at(-dy, flip)).wait_recv()


def finish(rows_in, meta, gain, rows_out, gates_out, scaled, sem):
    n_exp, _, width = rows_in.shape
    head = RAW * COLS
    rest = pltpu.make_async_copy(
        rows_in.at[:, :, head:width], rows_out.at[:, :, head:width], sem.at[0]
    )
    rest.start()
    wide = rows_in[:, :, 0:head].astype(F32) * meta[:, 0:CAP, 0:1]
    scaled[...] = (wide * gain[:, 0:head].reshape(1, 1, head)).astype(BF16)
    first = pltpu.make_async_copy(scaled, rows_out.at[:, :, 0:head], sem.at[1])
    first.start()
    lane = iota((CAP, n_exp), 1)
    gates = jnp.zeros((CAP, n_exp), F32)
    for j in range(n_exp):
        gates = jnp.where(lane == j, meta[j, CAP : 2 * CAP, 0:n_exp], gates)
    gates_out[...] = gates.astype(BF16)
    rest.wait()
    first.wait()


def on_device(
    sizes, queries, keys_in, values, decay_rate, out_weight, residual, norm_gain, router, expert_ids
):
    n_sec, n_ctx, n_exp = sizes
    length, inner_width = queries.shape[1:]
    width = out_weight.shape[-1]
    tok = residual.shape[1]
    n_y = n_exp // 2
    half = n_y // 2
    cols = COLS
    chunks = width // cols
    rows = HEAD_DEV * HEAD_DIM // n_ctx
    any_space = pl.BlockSpec(memory_space=pl.ANY)
    dma = pltpu.SemaphoreType.DMA
    vmem_space = pl.BlockSpec(memory_space=pltpu.VMEM)
    slots, meta = pl.pallas_call(
        functools.partial(kernel, (n_sec, n_ctx, n_exp, length, width, cols)),
        out_shape=(
            jax.ShapeDtypeStruct((n_exp, CAP, width), BF16),
            jax.ShapeDtypeStruct((n_exp, 8, 128), F32),
        ),
        in_specs=[pl.BlockSpec(memory_space=pltpu.HBM)] * 9,
        out_specs=(any_space, any_space),
        scratch_shapes=[
            pltpu.VMEM((length, inner_width), BF16),
            pltpu.VMEM((length, inner_width), BF16),
            pltpu.VMEM((length, inner_width), BF16),
            pltpu.VMEM((HEAD_DEV, length), F32),
            pltpu.VMEM((tok, width), BF16),
            pltpu.VMEM((1, width), F32),
            pltpu.VMEM((n_exp, width), BF16),
            pltpu.VMEM((2, tok), jnp.int32),
            pltpu.VMEM((2, inner_width, width), BF16),
            pltpu.VMEM((length, inner_width), F32),
            pltpu.VMEM((2, n_y * tok, inner_width), BF16),
            pltpu.VMEM((n_y * tok, inner_width), BF16),
            pltpu.VMEM((chunks, n_y, tok, cols), F32),
            pltpu.VMEM((n_ctx, rows + 16, HEAD_DIM), BF16),
            pltpu.VMEM((n_ctx, rows + 16, HEAD_DIM), BF16),
            pltpu.VMEM((n_ctx, rows, HEAD_DIM), BF16),
            pltpu.VMEM((n_ctx, rows, HEAD_DIM), BF16),
            pltpu.VMEM((2, half, chunks, tok, cols), BF16),
            pltpu.VMEM((2, half, chunks, tok, cols), BF16),
            pltpu.VMEM((chunks, tok, cols), BF16),
            pltpu.VMEM((chunks, tok, cols), BF16),
            pltpu.VMEM((chunks, n_exp, CAP, cols), BF16),
            pltpu.VMEM((n_exp * 8, tok), BF16),
            pltpu.VMEM((tok, 128), F32),
            pltpu.VMEM((n_exp, 8, 128), F32),
            dma((9,)),
            dma((chunks + 1,)),
            dma((chunks + 1,)),
            dma((2, n_ctx)),
            dma((2, n_ctx)),
            dma((2, half, chunks)),
            dma((2, half, chunks)),
            dma((2, 2, chunks, 2)),
            dma((2, 2, chunks, 2)),
            dma((chunks,)),
            dma((chunks,)),
            dma((chunks, n_exp)),
            dma((chunks, n_exp)),
            dma((n_exp,)),
            dma((n_exp,)),
            dma((chunks + 1,)),
        ],
        compiler_params=pltpu.CompilerParams(
            collective_id=0, has_side_effects=True, vmem_limit_bytes=VMEM_MIB * 2**20
        ),
    )(
        *(
            pltpu.with_memory_space_constraint(x, pltpu.HBM)
            for x in (
                queries[0],
                keys_in[0],
                values[0],
                decay_rate[0],
                out_weight[0],
                residual[0],
                norm_gain,
                router[0].T,
                expert_ids[0].T,
            )
        )
    )
    rows_out, gates = pl.pallas_call(
        finish,
        out_shape=(
            jax.ShapeDtypeStruct((n_exp, CAP, width), BF16),
            jax.ShapeDtypeStruct((CAP, n_exp), BF16),
        ),
        in_specs=[vmem_space] * 3,
        out_specs=(any_space, vmem_space),
        scratch_shapes=[pltpu.VMEM((n_exp, CAP, RAW * cols), BF16), dma((2,))],
        compiler_params=pltpu.CompilerParams(vmem_limit_bytes=8 * 2**20),
    )(slots, meta, norm_gain)
    return (rows_out[None, None, None], gates.T[None, None, None])


def solution(mesh):
    sizes = tuple(mesh.shape[a] for a in ("section", "ctx", "exp"))
    placed = (
        P("section", "ctx", "exp"),
        P("section", "ctx", "exp"),
        P("section", "ctx", "exp"),
        P("section", "exp", "ctx"),
        P("section", "exp", None),
        P("section", ("ctx", "exp"), None),
        P("section", None),
        P("section", None, None),
        P("section", ("ctx", "exp"), None),
    )
    return jax.shard_map(
        functools.partial(on_device, sizes),
        mesh=mesh,
        in_specs=placed,
        out_specs=(
            P("section", "ctx", "exp", None, None, None),
            P("section", "ctx", "exp", None, None),
        ),
        check_vma=False,
    )
```

time: 92.2 us -> 81.9 us (0.89)
  local copies, waits for them, and re-layouts: 10.7 us -> 0.01 us
  Pallas kernels: 78 us -> 81 us
  other arithmetic: 2.35 us -> 0 us
    unnamed x3 -> x2, local copies, waits for them, and re-layouts: 4.37 us -> 0.01 us
    slice x4 -> x0, local copies, waits for them, and re-layouts: 2.47 us -> none  [the longest x2 1.53 us: on_device(): gates = meta[:, CAP:2 * CAP, 0].astype(BF16)]
    convert_element_type x1 -> x0, local copies, waits for them, and re-layouts: 1.68 us -> none  [on_device(): rows_in = raw.reshape(n_exp, chunks, 4, CAP, cols).astype(F32)]
    pallas_call x1, Pallas kernels: 78 us -> 79.6 us  [on_device(): pl.pallas_call(functools.partial(kernel, (n_sec, n_ctx, n_exp, length, wi...]
    pallas_call x0 -> x1, Pallas kernels: none -> 1.48 us  [on_device(): pl.pallas_call(finish, out_shape=(jax.ShapeDtypeStruct((n_exp, CAP, width...]
    unnamed x1 -> x0, other arithmetic: 1.44 us -> none
    squeeze x1 -> x0, local copies, waits for them, and re-layouts: 1.35 us -> none  [on_device(): expert_ids[0]]
where the time goes in v2:
time: 81.9 us; the launch traced here: 81.7 us
  Pallas kernels  81 us (99%)
    pallas_call x1, Pallas kernels, on_device(): pl.pallas_call(functools.partial(kernel, (n_sec, n_ctx, n_exp, length, wi...  79.6 us

profile of v2, /device:TPU:1, one launch (start us, length us, event | category | flops | bytes accessed | tf_op | source)
XLA Modules:
  0.0 81.7 jit_solution(17310059293670154497)
XLA Ops:
  0.6 0.0 copy-start
  0.6 79.6 %shard_map.104 = (bf16[16,4,6144]{2,1,0:T(4,128)(2,1)S(1)}, f32[16,8,128]{2,1,0:T(8,128)S(1)}) custom-call(bf16[256,512]{1,0:T(8,128)(2,1)} %bitcast.17, bf16[256,512]{1,0:T(8,128)(2,1)} %bitcast.18, bf16[256,512]{1,0:T(8,128)(2,1)} %bitcast.19, f32[4,256]{1,0:T(4,128)} %bitcast.22, bf16[512,6144]{1,0:T(8,128)(2,1)} %bitcast.16, bf16[16,6144]{1,0:T(8,128)(2,1)} %bitcast.20, ...), custom_call_target="tpu_custom_call" | custom-call | tf_op jit(solution)/shard_map/pallas_call | solution.py:530
  80.2 0.0 copy-done
  80.2 1.5 %shard_map.105 = (bf16[16,4,6144]{2,1,0:T(4,128)(2,1)}, bf16[4,16]{1,0:T(4,128)(2,1)}) custom-call(bf16[16,4,6144]{2,1,0:T(4,128)(2,1)S(1)} %get-tuple-element.6.rows_in, f32[16,8,128]{2,1,0:T(8,128)S(1)} %get-tuple-element.7.meta, f32[1,6144]{1,0:T(1,128)S(1)} %copy-done), custom_call_target="tpu_custom_call" | custom-call | tf_op jit(solution)/shard_map/pallas_call | solution.py:600
Async XLA Ops:
  0.6 79.6 %copy-start = (f32[1,6144]{1,0:T(1,128)S(1)}, f32[1,6144]{1,0:T(1,128)}, u32[]{:S(2)}) copy-start(f32[1,6144]{1,0:T(1,128)} %gain.1) | copy-start | bytes 73732

commit v3 on v2

--- a/solution.py
+++ b/solution.py
@@ -11,8 +11,8 @@
 HEAD_DEV = 4
 CAP = 4
 EPS = 1e-05
-COLS = 1024
-RAW = 2
+COLS = 1536
+RAW = 1
 VMEM_MIB = 36
 MESH = pl.DeviceIdType.MESH
 F32 = jnp.float32
@@ -83,8 +83,6 @@
     z_recv,
     ring_send,
     ring_recv,
-    half_send,
-    half_recv,
     shift_send,
     shift_recv,
     slot_send,
@@ -186,7 +184,13 @@
     def z_copy(phase, d, out, into, theirs):
         peer = (ctx + d) % n_ctx
         return remote(
-            out.at[peer], into.at[theirs], z_send.at[phase, d], z_recv.at[phase, d], ctx=peer
+            out.at[peer], into.at[theirs], z_send.at[phase], z_recv.at[phase], ctx=peer
+        )
+
+    def z_all(phase, out, into):
+        span = pl.ds(0, n_ctx - 1)
+        return remote(
+            out.at[span], into.at[span], z_send.at[phase], z_recv.at[phase], ctx=(ctx + 1) % n_ctx
         )
 
     if n_ctx > 1:
@@ -199,7 +203,7 @@
         return remote(
             w_hbm.at[:, columns(i)],
             weights.at[1, :, columns(i)],
-            pair_send.at[i],
+            pair_send.at[0],
             pair_recv.at[i],
             exp=exp_at(0, 1),
         )
@@ -233,8 +237,7 @@
     picks[...] = (codes == line.astype(F32)).astype(BF16)
 
     if n_ctx > 1:
-        for d in far_first:
-            z_copy(0, d, state_out, state_in, (ctx - d + n_ctx) % n_ctx).wait_recv()
+        z_all(0, state_out, state_in).wait_recv()
         carried = jnp.zeros((rows, HEAD_DIM), F32)
         for n in range(n_ctx):
             scan_out[n] = carried.astype(BF16)
@@ -245,8 +248,7 @@
         for d in far_first:
             z_copy(1, d, scan_out, scan_in, ctx).start()
         scan_in[ctx] = scan_out[ctx]
-        for d in far_first:
-            z_copy(1, d, scan_out, scan_in, (ctx - d + n_ctx) % n_ctx).wait_recv()
+        z_all(1, scan_out, scan_in).wait_recv()
 
     grow = jnp.exp(b_col)
     for h in range(HEAD_DEV):
@@ -261,7 +263,7 @@
         for c in range(2):
             attended[c, :, at] = split[:, c].reshape(n_y * tok, HEAD_DIM)
     pair_a = remote(
-        attended.at[1 - core], att_in, pair_send.at[chunks], pair_recv.at[chunks], exp=exp_at(0, 1)
+        attended.at[1 - core], att_in, pair_send.at[1], pair_recv.at[chunks], exp=exp_at(0, 1)
     )
     pair_a.start()
     loads[5].wait()
@@ -274,7 +276,7 @@
         return remote(
             ring_out.at[way, step, i],
             ring_in.at[way, step, i],
-            ring_send.at[way, step, i],
+            ring_send.at[2],
             ring_recv.at[way, step, i],
             exp=left if way else right,
         )
@@ -284,18 +286,16 @@
         return remote(
             ring_out.at[way, step, i, :, part],
             ring_in.at[way, step, i, :, part],
-            half_send.at[way, step, i, p],
-            half_recv.at[way, step, i, p],
+            ring_send.at[step],
+            ring_recv.at[way, step, i],
             exp=left if way else right,
         )
 
     def arrived(way, step, i):
-        if step > 1:
+        if step > 0:
             ring_copy(way, step, i).wait_recv()
         else:
-            for p in range(2):
-                if step == 1 or p == way:
-                    half_copy(way, step, i, p).wait_recv()
+            half_copy(way, 0, i, way).wait_recv()
 
     def dest(way, step):
         away = half - step
@@ -358,25 +358,26 @@
         return remote(
             shift_out.at[i],
             shift_in.at[i],
-            shift_send.at[i],
+            shift_send.at[0],
             shift_recv.at[i],
             section=(sec + 1) % n_sec,
         )
 
-    def slot_copy(i, dy, flip, sender):
+    groups = (pl.ds(0, RAW * cols), pl.ds(RAW * cols, width - RAW * cols))
+
+    def slot_copy(g, dy, flip):
         peer = exp_at(dy, flip)
-        k = dy * 2 + flip
         return remote(
-            placed.at[i, peer],
-            rows_out.at[sender, :, columns(i)],
-            slot_send.at[i, k],
-            slot_recv.at[i, k],
+            placed.at[peer, :, groups[g]],
+            rows_out.at[exp, :, groups[g]],
+            slot_send.at[g],
+            slot_recv.at[g],
             exp=peer,
         )
 
-    def own_copy(i):
+    def own_copy(g):
         return pltpu.make_async_copy(
-            placed.at[i, exp], rows_out.at[exp, :, columns(i)], own_sem.at[i]
+            placed.at[exp, :, groups[g]], rows_out.at[exp, :, groups[g]], own_sem.at[g]
         )
 
     order = sorted(range(1, n_y), key=lambda d: -min(d, n_y - d)) + [0]
@@ -384,10 +385,12 @@
 
     def place(i):
         slots = jnp.dot(picks[...], shift_in[i], preferred_element_type=F32)
-        placed[i] = slots.reshape(n_exp, 8, cols)[:, 0:CAP].astype(BF16)
+        placed[:, :, columns(i)] = slots.reshape(n_exp, 8, cols)[:, 0:CAP].astype(BF16)
+
+    def send_slots(g):
         for dy, flip in others:
-            slot_copy(i, dy, flip, exp).start()
-        own_copy(i).start()
+            slot_copy(g, dy, flip).start()
+        own_copy(g).start()
 
     squares[...] = jnp.zeros_like(squares)
 
@@ -420,6 +423,10 @@
             now = i - 2
             add_squares(now)
             place(now)
+
+            @pl.when(now == RAW - 1)
+            def _():
+                send_slots(0)
 
     @pl.loop(RAW, chunks)
     def _(i):
@@ -447,49 +454,67 @@
     info = jnp.sum(info, axis=-1, keepdims=True)
     meta_out[...] = jnp.broadcast_to(info, (slot_rows, 128)).reshape(n_exp, 8, 128)
 
-    def meta_copy(dy, flip, sender):
+    for dy, flip in others:
         peer = exp_at(dy, flip)
-        k = dy * 2 + flip
-        return remote(
-            meta_out.at[peer], meta_in.at[sender], meta_send.at[k], meta_recv.at[k], exp=peer
-        )
-
-    for dy, flip in others:
-        meta_copy(dy, flip, exp).start()
-    own_meta = pltpu.make_async_copy(meta_out.at[exp], meta_in.at[exp], own_sem.at[chunks])
+        remote(
+            meta_out.at[peer], meta_in.at[exp], meta_send.at[0], meta_recv.at[0], exp=peer
+        ).start()
+    own_meta = pltpu.make_async_copy(meta_out.at[exp], meta_in.at[exp], own_sem.at[2])
     own_meta.start()
 
     @pl.loop(RAW, chunks)
     def _(i):
         place(i)
 
+    send_slots(1)
+
     pair_a.wait_send()
-    for d in far_first:
-        for phase, (out, into) in enumerate(((state_out, state_in), (scan_out, scan_in))):
-            z_copy(phase, d, out, into, ctx).wait_send()
-
-    @pl.loop(0, chunks)
-    def _(i):
-        pair_w(i).wait_send()
-        for way in range(2):
-            for step in range(half):
-                if step > 1:
-                    ring_copy(way, step, i).wait_send()
-                else:
-                    for p in range(2):
-                        if step == 1 or p == way:
-                            half_copy(way, step, i, p).wait_send()
-        if n_sec > 1:
-            shift_copy(i).wait_send()
-        own_copy(i).wait()
-        for dy, flip in others:
-            slot_copy(i, dy, flip, exp).wait_send()
-            slot_copy(i, dy, flip, exp_at(-dy, flip)).wait_recv()
-
+    remote(
+        w_hbm, weights.at[1], pair_send.at[0], pair_recv.at[0], exp=exp_at(0, 1)
+    ).wait_send()
+    if n_ctx > 1:
+        z_all(0, state_out, state_in).wait_send()
+        z_all(1, scan_out, scan_in).wait_send()
+
+    for step in range(min(half, 2)):
+        sent = ring_out.at[0, 0] if step == 0 else ring_out.at[:, 1]
+        into = ring_in.at[0, 0] if step == 0 else ring_in.at[:, 1]
+        remote(sent, into, ring_send.at[step], ring_recv.at[0, 0, 0], exp=right).wait_send()
+    if half > 2:
+        later = pl.ds(2, half - 2)
+        remote(
+            ring_out.at[:, later],
+            ring_in.at[:, later],
+            ring_send.at[2],
+            ring_recv.at[0, 0, 0],
+            exp=right,
+        ).wait_send()
+    if n_sec > 1:
+        remote(
+            shift_out, shift_in, shift_send.at[0], shift_recv.at[0], section=(sec + 1) % n_sec
+        ).wait_send()
     own_meta.wait()
-    for dy, flip in others:
-        meta_copy(dy, flip, exp).wait_send()
-        meta_copy(dy, flip, exp_at(-dy, flip)).wait_recv()
+    meta_all = remote(
+        meta_out.at[pl.ds(0, n_exp - 1)],
+        meta_in.at[pl.ds(0, n_exp - 1)],
+        meta_send.at[0],
+        meta_recv.at[0],
+        exp=right,
+    )
+    meta_all.wait_send()
+    meta_all.wait_recv()
+    for g in range(2):
+        own_copy(g).wait()
+        most = pl.ds(0, n_exp - 1)
+        slots_all = remote(
+            placed.at[most, :, groups[g]],
+            rows_out.at[most, :, groups[g]],
+            slot_send.at[g],
+            slot_recv.at[g],
+            exp=right,
+        )
+        slots_all.wait_send()
+        slots_all.wait_recv()
 
 
 def finish(rows_in, meta, gain, rows_out, gates_out, scaled, sem):
@@ -557,26 +582,24 @@
             pltpu.VMEM((2, half, chunks, tok, cols), BF16),
             pltpu.VMEM((chunks, tok, cols), BF16),
             pltpu.VMEM((chunks, tok, cols), BF16),
-            pltpu.VMEM((chunks, n_exp, CAP, cols), BF16),
+            pltpu.VMEM((n_exp, CAP, width), BF16),
             pltpu.VMEM((n_exp * 8, tok), BF16),
             pltpu.VMEM((tok, 128), F32),
             pltpu.VMEM((n_exp, 8, 128), F32),
             dma((9,)),
+            dma((2,)),
             dma((chunks + 1,)),
-            dma((chunks + 1,)),
-            dma((2, n_ctx)),
-            dma((2, n_ctx)),
+            dma((2,)),
+            dma((2,)),
+            dma((3,)),
             dma((2, half, chunks)),
-            dma((2, half, chunks)),
-            dma((2, 2, chunks, 2)),
-            dma((2, 2, chunks, 2)),
+            dma((1,)),
             dma((chunks,)),
-            dma((chunks,)),
-            dma((chunks, n_exp)),
-            dma((chunks, n_exp)),
-            dma((n_exp,)),
-            dma((n_exp,)),
-            dma((chunks + 1,)),
+            dma((2,)),
+            dma((2,)),
+            dma((1,)),
+            dma((1,)),
+            dma((3,)),
         ],
         compiler_params=pltpu.CompilerParams(
             collective_id=0, has_side_effects=True, vmem_limit_bytes=VMEM_MIB * 2**20

time: 81.9 us -> 77.2 us (0.943)
  Pallas kernels: 81 us -> 76.3 us
    pallas_call x1, Pallas kernels: 79.6 us -> 74.8 us  [on_device(): pl.pallas_call(functools.partial(kernel, (n_sec, n_ctx, n_exp, length, wi...]
where the time goes in v3:
time: 77.2 us; the launch traced here: 77 us
  Pallas kernels  76.3 us (99%)
    pallas_call x1, Pallas kernels, on_device(): pl.pallas_call(functools.partial(kernel, (n_sec, n_ctx, n_exp, length, wi...  74.8 us

profile of v3, /device:TPU:1, one launch (start us, length us, event | category | flops | bytes accessed | tf_op | source)
XLA Modules:
  0.0 77.0 jit_solution(14562885973973887779)
XLA Ops:
  0.6 0.0 copy-start
  0.6 74.8 %shard_map.104 = (bf16[16,4,6144]{2,1,0:T(4,128)(2,1)S(1)}, f32[16,8,128]{2,1,0:T(8,128)S(1)}) custom-call(bf16[256,512]{1,0:T(8,128)(2,1)} %bitcast.17, bf16[256,512]{1,0:T(8,128)(2,1)} %bitcast.18, bf16[256,512]{1,0:T(8,128)(2,1)} %bitcast.19, f32[4,256]{1,0:T(4,128)} %bitcast.22, bf16[512,6144]{1,0:T(8,128)(2,1)} %bitcast.16, bf16[16,6144]{1,0:T(8,128)(2,1)} %bitcast.20, ...), custom_call_target="tpu_custom_call" | custom-call | tf_op jit(solution)/shard_map/pallas_call | solution.py:555
  75.5 0.0 copy-done
  75.5 1.5 %shard_map.105 = (bf16[16,4,6144]{2,1,0:T(4,128)(2,1)}, bf16[4,16]{1,0:T(4,128)(2,1)}) custom-call(bf16[16,4,6144]{2,1,0:T(4,128)(2,1)S(1)} %get-tuple-element.6.rows_in, f32[16,8,128]{2,1,0:T(8,128)S(1)} %get-tuple-element.7.meta, f32[1,6144]{1,0:T(1,128)S(1)} %copy-done), custom_call_target="tpu_custom_call" | custom-call | tf_op jit(solution)/shard_map/pallas_call | solution.py:623
Async XLA Ops:
  0.6 74.9 %copy-start = (f32[1,6144]{1,0:T(1,128)S(1)}, f32[1,6144]{1,0:T(1,128)}, u32[]{:S(2)}) copy-start(f32[1,6144]{1,0:T(1,128)} %gain.1) | copy-start | bytes 73732

commit v4 on v3

--- a/solution.py
+++ b/solution.py
@@ -128,10 +128,8 @@
 
     barrier = pltpu.get_barrier_semaphore()
     partners = 0
-    for d in range(1, n_exp):
-        pl.semaphore_signal(
-            barrier, inc=1, device_id={"exp": (exp + d) % n_exp}, device_id_type=MESH
-        )
+    for who in (exp_at(0,1), exp_at(1), exp_at(-1)):
+        pl.semaphore_signal(barrier, inc=1, device_id={"exp": who}, device_id_type=MESH)
         partners += 1
     for d in range(1, n_ctx):
         pl.semaphore_signal(

time: 77.2 us -> 76.8 us (level)
  no operation moved by 1% of the time
where the time goes in v4:
time: 76.8 us; the launch traced here: 76.6 us
  Pallas kernels  76 us (99%)
    pallas_call x1, Pallas kernels, on_device(): pl.pallas_call(functools.partial(kernel, (n_sec, n_ctx, n_exp, length, wi...  74.5 us

profile of v4, /device:TPU:1, one launch (start us, length us, event | category | flops | bytes accessed | tf_op | source)
XLA Modules:
  0.0 76.6 jit_solution(104887892280053961)
XLA Ops:
  0.6 0.0 copy-start
  0.6 74.5 %shard_map.104 = (bf16[16,4,6144]{2,1,0:T(4,128)(2,1)S(1)}, f32[16,8,128]{2,1,0:T(8,128)S(1)}) custom-call(bf16[256,512]{1,0:T(8,128)(2,1)} %bitcast.17, bf16[256,512]{1,0:T(8,128)(2,1)} %bitcast.18, bf16[256,512]{1,0:T(8,128)(2,1)} %bitcast.19, f32[4,256]{1,0:T(4,128)} %bitcast.22, bf16[512,6144]{1,0:T(8,128)(2,1)} %bitcast.16, bf16[16,6144]{1,0:T(8,128)(2,1)} %bitcast.20, ...), custom_call_target="tpu_custom_call" | custom-call | tf_op jit(solution)/shard_map/pallas_call | solution.py:553
  75.2 0.0 copy-done
  75.2 1.5 %shard_map.105 = (bf16[16,4,6144]{2,1,0:T(4,128)(2,1)}, bf16[4,16]{1,0:T(4,128)(2,1)}) custom-call(bf16[16,4,6144]{2,1,0:T(4,128)(2,1)S(1)} %get-tuple-element.6.rows_in, f32[16,8,128]{2,1,0:T(8,128)S(1)} %get-tuple-element.7.meta, f32[1,6144]{1,0:T(1,128)S(1)} %copy-done), custom_call_target="tpu_custom_call" | custom-call | tf_op jit(solution)/shard_map/pallas_call | solution.py:621
Async XLA Ops:
  0.6 74.5 %copy-start = (f32[1,6144]{1,0:T(1,128)S(1)}, f32[1,6144]{1,0:T(1,128)}, u32[]{:S(2)}) copy-start(f32[1,6144]{1,0:T(1,128)} %gain.1) | copy-start | bytes 73732
